TPU v7x, 32 devices: a whole 2x2x4 slice. The times are simulated.
32 devices in a mesh: level: 8 (over y, x, core), row: 4 (over z).
Axes of the slice: x: 2, y: 2, z: 4, core: 2. Of those that a mesh axis runs over, the one named last changes fastest.
Arguments:
- right_side: float32 [64, 32, 128], P('level'), may hold values from -6 to 6
- inverses: float32 [64, 128, 128], P('level'), as said below
- blocks: float32 [64, 8, 128, 128], P('level', 'row'), may hold values from -0.125 to 0.125
- sources: int32 [64, 8], P('level', 'row'), may hold values from -1 to 55, as said below
Outputs:
- solved: float32 [64, 32, 128], P('level')
Inputs may be any that keep to these rules, and one draw needn't show every extreme that they name: `sources`: the supernodes form an elimination tree: every supernode below the top level has one parent on the next level, and every supernode above level 0 has exactly one child. The entries of supernode t are its 8 highest-numbered descendants in that tree, distinct and in falling order, followed by -1 for empty slots; the supernodes of level 0 have only empty slots. `inverses`: lower triangular.
All inputs are finite; a program needn't handle non-finite values.
Results may differ from a plain program's by a relative error of at most 0.0001.
Values sent between devices are 32-bit elements; how exact they have to be, the bound alone decides.
No kernel may reach another device: no remote copies, remote signals or barrier semaphores. Data moves between devices by JAX's collectives and lax.ppermute only.
A program may use at most 64 MiB of HBM per device.

v0:
```python
import jax
import jax.numpy as jnp
from jax import lax
from jax.sharding import PartitionSpec as P


def spread(value, axis, source):
    kept = jnp.where(lax.axis_index(axis) == source, value, 0).astype(value.dtype)
    return lax.psum(kept, axis)


def per_device(right_side, inverses, blocks, sources):
    highest = lax.Precision.HIGHEST
    sn_count = right_side.shape[0]
    my_level = lax.axis_index("level")
    levels = lax.axis_size("level")

    def advance(level_now, carry):
        updates, solved = carry
        mine = my_level == level_now
        totals = lax.psum(updates, "row")
        own = jnp.einsum("snw,svw->snv", right_side - totals, inverses, precision=highest)
        current = spread(own, "level", level_now)
        solved = jnp.where(mine, current, solved)
        wanted = level_now * sn_count + jnp.arange(sn_count, dtype=jnp.int32)
        select = (sources[:, :, None] == wanted[None, None, :]).astype(jnp.float32)
        picked = jnp.einsum("srk,knw->srnw", select, current, precision=highest)
        updates = updates + jnp.einsum("srnw,srwv->snv", picked, blocks, precision=highest)
        return (updates, solved)

    empty = jnp.zeros(right_side.shape, jnp.float32)
    updates, solved = lax.fori_loop(0, levels, advance, (empty, empty))
    return solved


def solution(mesh):
    return jax.shard_map(
        per_device,
        mesh=mesh,
        in_specs=(
            P("level", None, None),
            P("level", None, None),
            P("level", "row", None, None),
            P("level", "row"),
        ),
        out_specs=P("level", None, None),
        check_vma=False,
    )
```

profile of v0, /device:TPU:30, one launch (start us, length us, event | category | flops | bytes accessed | tf_op | source)
XLA Modules:
  0.0 778.0 jit_solution(18321583379033328239)
XLA Ops:
  7.2 763.6 %while.18 = (s32[]{:T(128)}, f32[8,32,128]{2,1,0:T(8,128)S(1)}, f32[8,32,128]{2,1,0:T(8,128)S(1)}, s32[8,2]{0,1:T(2,128)S(1)}, f32[8,32,128]{2,1,0:T(8,128)}, /*...) while((s32[]{:T(128)}, f32[8,32,128]{2,1,0:T(8,128)S(1)}, ...), condition=%wide.region_3.4_spmd.clone, body=%wide.region_0.3_spmd.clone.sunk | while | flops 157548688 | bytes 10355576 | solution.py:32
  8.1 36.6 %all-reduce.3.cloned.1.call-done = f32[8,32,128]{2,1,0:T(8,128)} async-done(((f32[8,32,128]{2,1,0:T(8,128)}), f32[8,32,128]{2,1,0:T(8,128)}) %all-reduce.3.cloned.1.call-update) | async-done | bytes 131088 | tf_op jit(solution)/shard_map/while/body/eval_jaxpr/psum | solution.py:21
  44.7 2.8 convolution_select_fusion.2
  47.5 53.0 %all-reduce.5.cloned.1.call-done = f32[8,32,128]{2,1,0:T(8,128)} async-done(((f32[8,32,128]{2,1,0:T(8,128)}), f32[8,32,128]{2,1,0:T(8,128)}) %all-reduce.5.cloned.1.call-update) | async-done | bytes 131088 | tf_op jit(solution)/shard_map/while/body/eval_jaxpr/psum | solution.py:9
  100.6 1.2 fusion.22
  103.7 36.6 %all-reduce.3.cloned.1.call-done = f32[8,32,128]{2,1,0:T(8,128)} async-done(((f32[8,32,128]{2,1,0:T(8,128)}), f32[8,32,128]{2,1,0:T(8,128)}) %all-reduce.3.cloned.1.call-update) | async-done | bytes 131088 | tf_op jit(solution)/shard_map/while/body/eval_jaxpr/psum | solution.py:21
  140.3 2.8 convolution_select_fusion.2
  143.2 52.9 %all-reduce.5.cloned.1.call-done = f32[8,32,128]{2,1,0:T(8,128)} async-done(((f32[8,32,128]{2,1,0:T(8,128)}), f32[8,32,128]{2,1,0:T(8,128)}) %all-reduce.5.cloned.1.call-update) | async-done | bytes 131088 | tf_op jit(solution)/shard_map/while/body/eval_jaxpr/psum | solution.py:9
  196.1 1.2 fusion.22
  199.2 36.3 %all-reduce.3.cloned.1.call-done = f32[8,32,128]{2,1,0:T(8,128)} async-done(((f32[8,32,128]{2,1,0:T(8,128)}), f32[8,32,128]{2,1,0:T(8,128)}) %all-reduce.3.cloned.1.call-update) | async-done | bytes 131088 | tf_op jit(solution)/shard_map/while/body/eval_jaxpr/psum | solution.py:21
  235.5 2.8 convolution_select_fusion.2
  238.4 52.9 %all-reduce.5.cloned.1.call-done = f32[8,32,128]{2,1,0:T(8,128)} async-done(((f32[8,32,128]{2,1,0:T(8,128)}), f32[8,32,128]{2,1,0:T(8,128)}) %all-reduce.5.cloned.1.call-update) | async-done | bytes 131088 | tf_op jit(solution)/shard_map/while/body/eval_jaxpr/psum | solution.py:9
  291.3 1.2 fusion.22
  294.4 36.6 %all-reduce.3.cloned.1.call-done = f32[8,32,128]{2,1,0:T(8,128)} async-done(((f32[8,32,128]{2,1,0:T(8,128)}), f32[8,32,128]{2,1,0:T(8,128)}) %all-reduce.3.cloned.1.call-update) | async-done | bytes 131088 | tf_op jit(solution)/shard_map/while/body/eval_jaxpr/psum | solution.py:21
  331.0 2.8 convolution_select_fusion.2
  333.9 53.0 %all-reduce.5.cloned.1.call-done = f32[8,32,128]{2,1,0:T(8,128)} async-done(((f32[8,32,128]{2,1,0:T(8,128)}), f32[8,32,128]{2,1,0:T(8,128)}) %all-reduce.5.cloned.1.call-update) | async-done | bytes 131088 | tf_op jit(solution)/shard_map/while/body/eval_jaxpr/psum | solution.py:9
  386.9 1.2 fusion.22
  390.0 36.6 %all-reduce.3.cloned.1.call-done = f32[8,32,128]{2,1,0:T(8,128)} async-done(((f32[8,32,128]{2,1,0:T(8,128)}), f32[8,32,128]{2,1,0:T(8,128)}) %all-reduce.3.cloned.1.call-update) | async-done | bytes 131088 | tf_op jit(solution)/shard_map/while/body/eval_jaxpr/psum | solution.py:21
  426.6 2.8 convolution_select_fusion.2
  429.5 52.9 %all-reduce.5.cloned.1.call-done = f32[8,32,128]{2,1,0:T(8,128)} async-done(((f32[8,32,128]{2,1,0:T(8,128)}), f32[8,32,128]{2,1,0:T(8,128)}) %all-reduce.5.cloned.1.call-update) | async-done | bytes 131088 | tf_op jit(solution)/shard_map/while/body/eval_jaxpr/psum | solution.py:9
  482.4 1.2 fusion.22
  485.5 36.6 %all-reduce.3.cloned.1.call-done = f32[8,32,128]{2,1,0:T(8,128)} async-done(((f32[8,32,128]{2,1,0:T(8,128)}), f32[8,32,128]{2,1,0:T(8,128)}) %all-reduce.3.cloned.1.call-update) | async-done | bytes 131088 | tf_op jit(solution)/shard_map/while/body/eval_jaxpr/psum | solution.py:21
  522.1 2.8 convolution_select_fusion.2
  525.0 52.9 %all-reduce.5.cloned.1.call-done = f32[8,32,128]{2,1,0:T(8,128)} async-done(((f32[8,32,128]{2,1,0:T(8,128)}), f32[8,32,128]{2,1,0:T(8,128)}) %all-reduce.5.cloned.1.call-update) | async-done | bytes 131088 | tf_op jit(solution)/shard_map/while/body/eval_jaxpr/psum | solution.py:9
  577.9 1.2 fusion.22
  581.0 36.6 %all-reduce.3.cloned.1.call-done = f32[8,32,128]{2,1,0:T(8,128)} async-done(((f32[8,32,128]{2,1,0:T(8,128)}), f32[8,32,128]{2,1,0:T(8,128)}) %all-reduce.3.cloned.1.call-update) | async-done | bytes 131088 | tf_op jit(solution)/shard_map/while/body/eval_jaxpr/psum | solution.py:21
  617.6 2.8 convolution_select_fusion.2
  620.5 52.9 %all-reduce.5.cloned.1.call-done = f32[8,32,128]{2,1,0:T(8,128)} async-done(((f32[8,32,128]{2,1,0:T(8,128)}), f32[8,32,128]{2,1,0:T(8,128)}) %all-reduce.5.cloned.1.call-update) | async-done | bytes 131088 | tf_op jit(solution)/shard_map/while/body/eval_jaxpr/psum | solution.py:9
  673.4 1.2 fusion.22
  676.5 36.3 %all-reduce.3.cloned.1.call-done = f32[8,32,128]{2,1,0:T(8,128)} async-done(((f32[8,32,128]{2,1,0:T(8,128)}), f32[8,32,128]{2,1,0:T(8,128)}) %all-reduce.3.cloned.1.call-update) | async-done | bytes 131088 | tf_op jit(solution)/shard_map/while/body/eval_jaxpr/psum | solution.py:21
  712.8 2.8 convolution_select_fusion.2
  715.7 52.9 %all-reduce.5.cloned.1.call-done = f32[8,32,128]{2,1,0:T(8,128)} async-done(((f32[8,32,128]{2,1,0:T(8,128)}), f32[8,32,128]{2,1,0:T(8,128)}) %all-reduce.5.cloned.1.call-update) | async-done | bytes 131088 | tf_op jit(solution)/shard_map/while/body/eval_jaxpr/psum | solution.py:9
  (135 shorter events, 17.6 us)
Async XLA Ops:
  7.2 94.6 %copy-start.1 = (f32[8,2,128,128]{3,2,1,0:T(8,128)S(1)}, f32[8,2,128,128]{3,2,1,0:T(8,128)}, u32[]{:S(2)}) copy-start(f32[8,2,128,128]{3,2,1,0:T(8,128)} %get-tuple-element.328) | copy-start | bytes 3145732 | tf_op jit(solution)/shard_map/while
  7.2 37.5 %all-reduce.3.cloned.1.call-start = ((), (), s32[]{:S(2)}) async-start(), calls=%async_computation | async-start | bytes 262144 | tf_op jit(solution)/shard_map/while/body/eval_jaxpr/psum | solution.py:21
  7.9 92.7 %all-reduce.5.cloned.1.call-start = ((), (), s32[]{:S(2)}) async-start(), calls=%async_computation.1 | async-start | bytes 262144 | tf_op jit(solution)/shard_map/while/body/eval_jaxpr/psum | solution.py:9
  100.6 1.2 copy-start
  102.8 94.5 %copy-start.1 = (f32[8,2,128,128]{3,2,1,0:T(8,128)S(1)}, f32[8,2,128,128]{3,2,1,0:T(8,128)}, u32[]{:S(2)}) copy-start(f32[8,2,128,128]{3,2,1,0:T(8,128)} %get-tuple-element.328) | copy-start | bytes 3145732 | tf_op jit(solution)/shard_map/while
  102.8 37.5 %all-reduce.3.cloned.1.call-start = ((), (), s32[]{:S(2)}) async-start(), calls=%async_computation | async-start | bytes 262144 | tf_op jit(solution)/shard_map/while/body/eval_jaxpr/psum | solution.py:21
  103.6 92.5 %all-reduce.5.cloned.1.call-start = ((), (), s32[]{:S(2)}) async-start(), calls=%async_computation.1 | async-start | bytes 262144 | tf_op jit(solution)/shard_map/while/body/eval_jaxpr/psum | solution.py:9
  196.1 1.2 copy-start
  198.3 94.2 %copy-start.1 = (f32[8,2,128,128]{3,2,1,0:T(8,128)S(1)}, f32[8,2,128,128]{3,2,1,0:T(8,128)}, u32[]{:S(2)}) copy-start(f32[8,2,128,128]{3,2,1,0:T(8,128)} %get-tuple-element.328) | copy-start | bytes 3145732 | tf_op jit(solution)/shard_map/while
  198.3 37.2 %all-reduce.3.cloned.1.call-start = ((), (), s32[]{:S(2)}) async-start(), calls=%async_computation | async-start | bytes 262144 | tf_op jit(solution)/shard_map/while/body/eval_jaxpr/psum | solution.py:21
  199.1 92.2 %all-reduce.5.cloned.1.call-start = ((), (), s32[]{:S(2)}) async-start(), calls=%async_computation.1 | async-start | bytes 262144 | tf_op jit(solution)/shard_map/while/body/eval_jaxpr/psum | solution.py:9
  291.3 1.2 copy-start
  293.5 94.7 %copy-start.1 = (f32[8,2,128,128]{3,2,1,0:T(8,128)S(1)}, f32[8,2,128,128]{3,2,1,0:T(8,128)}, u32[]{:S(2)}) copy-start(f32[8,2,128,128]{3,2,1,0:T(8,128)} %get-tuple-element.328) | copy-start | bytes 3145732 | tf_op jit(solution)/shard_map/while
  293.5 37.5 %all-reduce.3.cloned.1.call-start = ((), (), s32[]{:S(2)}) async-start(), calls=%async_computation | async-start | bytes 262144 | tf_op jit(solution)/shard_map/while/body/eval_jaxpr/psum | solution.py:21
  294.3 92.6 %all-reduce.5.cloned.1.call-start = ((), (), s32[]{:S(2)}) async-start(), calls=%async_computation.1 | async-start | bytes 262144 | tf_op jit(solution)/shard_map/while/body/eval_jaxpr/psum | solution.py:9
  386.9 1.2 copy-start
  389.1 94.5 %copy-start.1 = (f32[8,2,128,128]{3,2,1,0:T(8,128)S(1)}, f32[8,2,128,128]{3,2,1,0:T(8,128)}, u32[]{:S(2)}) copy-start(f32[8,2,128,128]{3,2,1,0:T(8,128)} %get-tuple-element.328) | copy-start | bytes 3145732 | tf_op jit(solution)/shard_map/while
  389.1 37.5 %all-reduce.3.cloned.1.call-start = ((), (), s32[]{:S(2)}) async-start(), calls=%async_computation | async-start | bytes 262144 | tf_op jit(solution)/shard_map/while/body/eval_jaxpr/psum | solution.py:21
  389.9 92.5 %all-reduce.5.cloned.1.call-start = ((), (), s32[]{:S(2)}) async-start(), calls=%async_computation.1 | async-start | bytes 262144 | tf_op jit(solution)/shard_map/while/body/eval_jaxpr/psum | solution.py:9
  482.4 1.2 copy-start
  484.6 94.5 %copy-start.1 = (f32[8,2,128,128]{3,2,1,0:T(8,128)S(1)}, f32[8,2,128,128]{3,2,1,0:T(8,128)}, u32[]{:S(2)}) copy-start(f32[8,2,128,128]{3,2,1,0:T(8,128)} %get-tuple-element.328) | copy-start | bytes 3145732 | tf_op jit(solution)/shard_map/while
  484.6 37.5 %all-reduce.3.cloned.1.call-start = ((), (), s32[]{:S(2)}) async-start(), calls=%async_computation | async-start | bytes 262144 | tf_op jit(solution)/shard_map/while/body/eval_jaxpr/psum | solution.py:21
  485.4 92.5 %all-reduce.5.cloned.1.call-start = ((), (), s32[]{:S(2)}) async-start(), calls=%async_computation.1 | async-start | bytes 262144 | tf_op jit(solution)/shard_map/while/body/eval_jaxpr/psum | solution.py:9
  577.9 1.2 copy-start
  580.1 94.5 %copy-start.1 = (f32[8,2,128,128]{3,2,1,0:T(8,128)S(1)}, f32[8,2,128,128]{3,2,1,0:T(8,128)}, u32[]{:S(2)}) copy-start(f32[8,2,128,128]{3,2,1,0:T(8,128)} %get-tuple-element.328) | copy-start | bytes 3145732 | tf_op jit(solution)/shard_map/while
  580.1 37.5 %all-reduce.3.cloned.1.call-start = ((), (), s32[]{:S(2)}) async-start(), calls=%async_computation | async-start | bytes 262144 | tf_op jit(solution)/shard_map/while/body/eval_jaxpr/psum | solution.py:21
  580.9 92.5 %all-reduce.5.cloned.1.call-start = ((), (), s32[]{:S(2)}) async-start(), calls=%async_computation.1 | async-start | bytes 262144 | tf_op jit(solution)/shard_map/while/body/eval_jaxpr/psum | solution.py:9
  673.4 1.2 copy-start
  675.6 94.2 %copy-start.1 = (f32[8,2,128,128]{3,2,1,0:T(8,128)S(1)}, f32[8,2,128,128]{3,2,1,0:T(8,128)}, u32[]{:S(2)}) copy-start(f32[8,2,128,128]{3,2,1,0:T(8,128)} %get-tuple-element.328) | copy-start | bytes 3145732 | tf_op jit(solution)/shard_map/while
  675.6 37.2 %all-reduce.3.cloned.1.call-start = ((), (), s32[]{:S(2)}) async-start(), calls=%async_computation | async-start | bytes 262144 | tf_op jit(solution)/shard_map/while/body/eval_jaxpr/psum | solution.py:21
  676.4 92.2 %all-reduce.5.cloned.1.call-start = ((), (), s32[]{:S(2)}) async-start(), calls=%async_computation.1 | async-start | bytes 262144 | tf_op jit(solution)/shard_map/while/body/eval_jaxpr/psum | solution.py:9
  768.6 1.2 copy-start
  (10 other events, 8.6 us)
Sparse Core Ops, SparseCore 0:
  10.3 34.3 all-reduce.2
  47.7 52.8 all-reduce.4
  105.9 34.3 all-reduce.2
  143.2 52.8 all-reduce.4
  201.1 34.3 all-reduce.2
  238.4 52.8 all-reduce.4
  296.6 34.3 all-reduce.2
  334.0 52.8 all-reduce.4
  392.3 34.3 all-reduce.2
  429.5 52.8 all-reduce.4
  487.8 34.3 all-reduce.2
  525.0 52.8 all-reduce.4
  583.3 34.3 all-reduce.2
  620.5 52.8 all-reduce.4
  678.5 34.3 all-reduce.2
  715.7 52.8 all-reduce.4
where the time goes:
time: 782 us; the launch traced here: 778 us
  waiting for transfers between devices  716 us (92%)
  matrix products  37.5 us (5%)
  between operations  13.1 us (2%)
    psum x8, waiting for transfers between devices, spread(): return lax.psum(kept, axis)  424 us
    psum x8, waiting for transfers between devices, advance(): totals = lax.psum(updates, 'row')  292 us
    dot_general x8, matrix products, advance(): jnp.einsum('snw,svw->snv', right_side - totals, inverses, precision=highest)  22 us
  transfers between devices with their start and end apart: 16, of which 16 were waited for; matrix products, arithmetic and copies ran while one was open for 0% of the time, Pallas kernels for 0%

commit v1 on v0

v1 whole, which is shorter than its diff:
```python
import functools

import jax
import jax.numpy as jnp
from jax import lax
from jax.experimental import pallas as pl
from jax.experimental.pallas import tpu as pltpu
from jax.sharding import PartitionSpec as P


F32 = jnp.float32
I32 = jnp.int32


def dot(x, w, dims=((1,), (0,))):
    return lax.dot_general(x, w, (dims, ((), ())), precision=lax.Precision.HIGHEST, preferred_element_type=F32)


def dot_t(x, w):
    return dot(x, w, ((1,), (1,)))


def emit(i, n, half, rows, msg, nat, ta, tb, xa, xb):
    msg[pl.ds(i * rows, rows), :] = xa
    msg[pl.ds((half + i) * rows, rows), :] = xb
    msg[pl.ds(2 * half * rows + i, 1), :] = jnp.broadcast_to(tb.astype(F32), (1, xa.shape[1]))
    nat[0, ta] = xa
    nat[1, tb] = xb


def first_kernel(n, half, rows, info, down, inv0, inv1, blk0, blk1, rhs0, rhs1, msg, nat):
    member = info[0]
    nat[...] = jnp.zeros_like(nat)
    msg[...] = jnp.zeros_like(msg)

    def run(inv_a, inv_b, blk_b, rhs_a, rhs_b):
        for i in range(half):
            tb = member * half + i
            ta = down[tb]
            xa = dot_t(rhs_a[ta], inv_a[ta])
            xb = dot_t(rhs_b[tb] - dot(xa, blk_b[tb, 0]), inv_b[tb])
            emit(i, n, half, rows, msg, nat, ta, tb, xa, xb)

    @pl.when(jnp.logical_and(info[1] == 1, member == 0))
    def _():
        run(inv0, inv1, blk1, rhs0, rhs1)

    @pl.when(jnp.logical_and(info[1] == 1, member == 1))
    def _():
        run(inv1, inv0, blk0, rhs1, rhs0)


def step_kernel(n, half, rows, count, info, up, *refs):
    member, active, solver = info[0], info[1], info[2]
    xs = refs[:count]
    acc_in, msg_in, nat_in = refs[count:count + 3]
    inv0, inv1, blk0, blk1, pre0, pre1, rhs0, rhs1, msg, nat = refs[count + 3:]

    @pl.when(active == 0)
    def _():
        msg[...] = msg_in[...]
        nat[...] = nat_in[...]

    def arrived(start, size):
        total = xs[0][pl.ds(start, size), :]
        for x in xs[1:]:
            total = total + x[pl.ds(start, size), :]
        return total

    def run(inv_a, inv_b, blk_a, blk_b, pre, rhs_a, rhs_b):
        nat[...] = jnp.zeros_like(nat)
        msg[...] = jnp.zeros_like(msg)
        ids = arrived(2 * half * rows, 8)
        for i in range(half):
            child = jnp.max(ids[i:i + 1]).astype(I32)
            ta, tb = up[0, child], up[1, child]
            sa, sb = arrived(i * rows, rows), arrived((half + i) * rows, rows)
            ua = acc_in[pl.ds(i * rows, rows), :] + dot(sa, blk_a[ta, 1]) + dot(sb, blk_a[ta, 0])
            ub = acc_in[pl.ds((half + i) * rows, rows), :] + dot(sa, pre[tb]) + dot(sb, blk_b[tb, 1])

            @pl.when(solver == 1)
            def _():
                xa = dot_t(rhs_a[ta] - ua, inv_a[ta])
                xb = dot_t(rhs_b[tb] - ub - dot(xa, blk_b[tb, 0]), inv_b[tb])
                emit(i, n, half, rows, msg, nat, ta, tb, xa, xb)

            @pl.when(solver == 0)
            def _():
                msg[pl.ds(i * rows, rows), :] = ua
                msg[pl.ds((half + i) * rows, rows), :] = ub

    @pl.when(jnp.logical_and(active == 1, member == 0))
    def _():
        run(inv0, inv1, blk0, blk1, pre1, rhs0, rhs1)

    @pl.when(jnp.logical_and(active == 1, member == 1))
    def _():
        run(inv1, inv0, blk1, blk0, pre0, rhs1, rhs0)


def call(kernel, n_smem, n_vmem, shapes):
    return pl.pallas_call(
        kernel,
        out_shape=shapes,
        in_specs=[pl.BlockSpec(memory_space=pltpu.SMEM)] * n_smem + [pl.BlockSpec(memory_space=pltpu.VMEM)] * n_vmem,
        out_specs=[pl.BlockSpec(memory_space=pltpu.VMEM)] * len(shapes),
        compiler_params=pltpu.CompilerParams(vmem_limit_bytes=32 * 1024 * 1024),
    )


def per_device(right_side, inverses, blocks, sources):
    n, rows, w = right_side.shape
    half = n // 2
    levels, planes = lax.axis_size("level"), lax.axis_size("row")
    stages = levels // 2
    level, plane = lax.axis_index("level"), lax.axis_index("row")
    member, stage = level % 2, level // 2

    def move(value, pairs):
        return lax.ppermute(value, ("level", "row"), [(a * planes + b, c * planes + d) for (a, b), (c, d) in pairs])

    def other(value):
        return lax.ppermute(value, "level", [(i, i ^ 1) for i in range(levels)])

    lower = [((l, p + 1), (l, p)) for l in range(3, levels, 2) for p in range(min(planes - 1, l // 2))]
    pre = move(blocks[:, 0], lower)

    sources_o = other(sources)
    inv_o, blk_o, rhs_o = other(inverses), other(blocks), other(right_side)

    src_a = jnp.where(member == 0, sources, sources_o)
    src_b = jnp.where(member == 0, sources_o, sources)
    offset = jnp.arange(n, dtype=I32)

    down = src_b[:, 0] % n
    info = jnp.stack([member, jnp.logical_and(stage == 0, plane == 0).astype(I32)]).astype(I32)
    shapes = [jax.ShapeDtypeStruct((2 * half * rows + 8, w), F32), jax.ShapeDtypeStruct((2, n, rows, w), F32)]
    msg, nat = call(functools.partial(first_kernel, n, half, rows), 2, 6, shapes)(
        info, jnp.clip(down, 0, n - 1), inverses, inv_o, blocks, blk_o, right_side, rhs_o)

    def inverse_map(column):
        hit = jnp.logical_and(column[:, None] >= 0, column[:, None] % n == offset[None, :])
        return jnp.sum(jnp.where(hit, offset[:, None], 0), axis=0).astype(I32)

    up = jnp.stack([inverse_map(src_a[:, 0]), inverse_map(src_b[:, 1])])
    pre_o = other(pre)
    acc = jnp.zeros_like(msg)
    for g in range(stages - 1):
        xs = [move(msg, [((2 * g + m, 0), (2 * (g + d) + m, d - 1)) for m in (0, 1)]) for d in range(1, stages - g)]
        back = [((2 * h + m, h - g), (2 * h + m, h - g - 1)) for h in range(g + 1, stages) for m in (0, 1)] if g else []
        if back:
            acc = move(msg, back)
        info = jnp.stack([member, (stage - 1 - plane == g).astype(I32), (plane == 0).astype(I32)]).astype(I32)
        msg, nat = call(functools.partial(step_kernel, n, half, rows, len(xs)), 2, len(xs) + 11, shapes)(
            info, up, *xs, acc, msg, nat, inverses, inv_o, blocks, blk_o, pre, pre_o, right_side, rhs_o)

    mine = lax.dynamic_index_in_dim(nat, member, 0, keepdims=False)
    theirs = lax.dynamic_index_in_dim(nat, 1 - member, 0, keepdims=False)
    solved = mine + other(theirs)
    out = jnp.where(plane == 0, solved, 0)
    for q in range(1, planes):
        out = out + move(solved, [((l, 0), (l, q)) for l in range(levels)])
    return out


def solution(mesh):
    return jax.shard_map(
        per_device,
        mesh=mesh,
        in_specs=(
            P("level", None, None),
            P("level", None, None),
            P("level", "row", None, None),
            P("level", "row"),
        ),
        out_specs=P("level", None, None),
        check_vma=False,
    )
```

time: 782 us -> 76.2 us (0.10)
  waiting for transfers between devices: 716 us -> 37.1 us
  matrix products: 37.5 us -> 0 us
  starting transfers between devices: 0.63 us -> 19.7 us
  between operations: 13.1 us -> 0.28 us
    psum x16 -> x0, waiting for transfers between devices: 716 us -> none  [the longest x8 424 us: spread(): return lax.psum(kept, axis)]
    dot_general x24 -> x0, matrix products: 37.5 us -> none  [the longest x8 22 us: advance(): jnp.einsum('snw,svw->snv', right_side - totals, inverses, precision=highest)]
    ppermute x0 -> x18, waiting for transfers between devices: none -> 37.1 us  [the longest x12 35.8 us: move(): lax.ppermute(value, ('level', 'row'), [(a * planes + b, c * planes + d) f...]
    ppermute x0 -> x18, starting transfers between devices: none -> 19.7 us  [the longest x12 12.6 us: move(): lax.ppermute(value, ('level', 'row'), [(a * planes + b, c * planes + d) f...]
    unnamed x4 -> x32, local copies, waits for them, and re-layouts: 1.33 us -> 10.2 us
  transfers between devices with their start and end apart: 16 -> 18, of which waited for: 16 -> 2; matrix products, arithmetic and copies ran while one was open for 0% -> 2% of each run, Pallas kernels for 0% -> 1%
where the time goes in v1:
time: 76.2 us; the launch traced here: 75.6 us
  waiting for transfers between devices  37.1 us (49%)
  starting transfers between devices  19.7 us (26%)
  local copies, waits for them, and re-layouts  11.3 us (15%)
  Pallas kernels  5.02 us (7%)
  other arithmetic  2.14 us (3%)
    ppermute x12, waiting for transfers between devices, move(): lax.ppermute(value, ('level', 'row'), [(a * planes + b, c * planes + d) f...  35.8 us
    ppermute x12, starting transfers between devices, move(): lax.ppermute(value, ('level', 'row'), [(a * planes + b, c * planes + d) f...  12.6 us
    unnamed x32, local copies, waits for them, and re-layouts  10.2 us
    ppermute x6, starting transfers between devices, other(): return lax.ppermute(value, 'level', [(i, i ^ 1) for i in range(levels)])  7.02 us
    pallas_call x3, Pallas kernels, per_device(): call(functools.partial(step_kernel, n, half, rows, len(xs)), 2, len(xs) +...  4.45 us
  transfers between devices with their start and end apart: 18, of which 2 were waited for; matrix products, arithmetic and copies ran while one was open for 2% of the time, Pallas kernels for 1%

profile of v1, /device:TPU:30, one launch (start us, length us, event | category | flops | bytes accessed | tf_op | source)
XLA Modules:
  0.0 75.6 jit_solution(6203878548224684774)
XLA Ops:
  1.0 1.1 %slice_bitcast_fusion = f32[8,128,128]{2,1,0:T(8,128)S(1)} fusion(f32[8,2,128,128]{3,2,1,0:T(8,128)} %refs_6_.3), kind=kLoop, calls=%fused_computation | loop fusion | bytes 1048576 | tf_op jit(solution)/shard_map/squeeze | solution.py:126
  2.1 1.5 %collective-permute-start.7 = (f32[8,128,128]{2,1,0:T(8,128)S(1)}, f32[8,128,128]{2,1,0:T(8,128)}, u32[]{:S(2)}, u32[]{:S(2)}) collective-permute-start(f32[8,128,128]{2,1,0:T(8,128)S(1)} %slice_bitcast_fusion), channel_id=1, source_target_pairs={{13,12},{21,20},{22,21},{29,28},{30,29},{31,30}} | collective-permute-start | bytes 1572872 | tf_op jit(solution)/shard_map/ppermute | solution.py:120
  3.7 0.7 copy-done.15
  4.4 5.9 %collective-permute-start.8 = (f32[8,128,128]{2,1,0:T(8,128)}, f32[8,128,128]{2,1,0:T(8,128)S(1)}, u32[]{:S(2)}, u32[]{:S(2)}) collective-permute-start(f32[8,128,128]{2,1,0:T(8,128)} %collective-permute-done.7.refs_10_.refs_9_.refs_8_), channel_id=1, source_target_pairs={{0,4},{4,0},{8,12},{12,8},{16,20},{20,16},{24,28},{28,24},{1,5},{5... | collective-permute-start | bytes 1572872 | tf_op jit(solution)/shard_map/ppermute | solution.py:123
  10.5 1.0 %copy-done.1 = f32[8,128,128]{2,1,0:T(8,128)S(1)} copy-done((f32[8,128,128]{2,1,0:T(8,128)S(1)}, f32[8,128,128]{2,1,0:T(8,128)}, u32[]{:S(2)}) %copy-start.1) | copy-done | bytes 524312
  11.5 0.9 %copy-done.6 = f32[8,32,128]{2,1,0:T(8,128)S(1)} copy-done((f32[8,32,128]{2,1,0:T(8,128)S(1)}, f32[8,32,128]{2,1,0:T(8,128)}, u32[]{:S(2)}) %copy-start.6) | copy-done | bytes 131096
  13.0 0.7 collective-permute-start.4
  13.7 0.7 collective-permute-start.5
  14.4 0.7 collective-permute-start.6
  15.2 1.3 %shard_map.47 = (f32[264,128]{1,0:T(8,128)S(1)}, f32[2,8,32,128]{3,2,1,0:T(8,128)S(1)}) custom-call(s32[3]{0:T(128)S(1)} %add_add_fusion.3.info, s32[2,8]{1,0:T(2,128)S(1)} %pad_add_fusion.up, f32[264,128]{1,0:T(8,128)S(1)} %collective-permute-done.4.refs_0_, f32[264,128]{1,0:T(8,128)S(1)} %collective-permute-done.5.refs_1_, ...), custom_call_target="tpu_custom_call" | custom-call | tf_op jit(solution)/shard_map/pallas_call | solution.py:154
  16.5 0.7 copy-done.10
  17.2 1.3 %collective-permute-start.10 = (f32[264,128]{1,0:T(8,128)S(1)}, f32[264,128]{1,0:T(8,128)}, u32[]{:S(2)}, u32[]{:S(2)}) collective-permute-start(f32[264,128]{1,0:T(8,128)S(1)} %get-tuple-element.14.refs_3_), channel_id=1, source_target_pairs={{8,25},{12,29}} | collective-permute-start | bytes 405512 | tf_op jit(solution)/shard_map/ppermute | solution.py:120
  18.6 1.3 %collective-permute-start.11 = (f32[264,128]{1,0:T(8,128)S(1)}, f32[264,128]{1,0:T(8,128)}, u32[]{:S(2)}, u32[]{:S(2)}) collective-permute-start(f32[264,128]{1,0:T(8,128)S(1)} %get-tuple-element.14.refs_3_), channel_id=1, source_target_pairs={{17,16},{21,20},{26,25},{30,29}} | collective-permute-start | bytes 405512 | tf_op jit(solution)/shard_map/ppermute | solution.py:120
  19.9 1.3 %collective-permute-start.9 = (f32[264,128]{1,0:T(8,128)S(1)}, f32[264,128]{1,0:T(8,128)}, u32[]{:S(2)}, u32[]{:S(2)}) collective-permute-start(f32[264,128]{1,0:T(8,128)S(1)} %get-tuple-element.14.refs_3_), channel_id=1, source_target_pairs={{8,16},{12,20}} | collective-permute-start | bytes 405512 | tf_op jit(solution)/shard_map/ppermute | solution.py:120
  21.9 1.0 %copy-done.4 = f32[8,128,128]{2,1,0:T(8,128)S(1)} copy-done((f32[8,128,128]{2,1,0:T(8,128)S(1)}, f32[8,128,128]{2,1,0:T(8,128)}, u32[]{:S(2)}) %copy-start.4) | copy-done | bytes 524312
  23.0 0.9 %copy-done.11 = f32[2,8,32,128]{3,2,1,0:T(8,128)S(1)} copy-done((f32[2,8,32,128]{3,2,1,0:T(8,128)S(1)}, f32[2,8,32,128]{3,2,1,0:T(8,128)}, u32[]{:S(2)}) %copy-start.11) | copy-done | bytes 262168
  23.9 0.9 %copy-done.14 = f32[264,128]{1,0:T(8,128)S(1)} copy-done((f32[264,128]{1,0:T(8,128)S(1)}, f32[264,128]{1,0:T(8,128)}, u32[]{:S(2)}) %copy-start.14) | copy-done | bytes 135192
  24.8 1.3 %shard_map.48 = (f32[264,128]{1,0:T(8,128)S(1)}, f32[2,8,32,128]{3,2,1,0:T(8,128)S(1)}) custom-call(s32[3]{0:T(128)S(1)} %add_add_fusion.2.info, s32[2,8]{1,0:T(2,128)S(1)} %pad_add_fusion.up, f32[264,128]{1,0:T(8,128)} %collective-permute-done.9.refs_0_, f32[264,128]{1,0:T(8,128)} %collective-permute-done.10.refs_1_, ...), custom_call_target="tpu_custom_call" | custom-call | tf_op jit(solution)/shard_map/pallas_call | solution.py:154
  26.1 0.7 copy-done.8
  26.8 1.3 %collective-permute-start.12 = (f32[264,128]{1,0:T(8,128)S(1)}, f32[264,128]{1,0:T(8,128)}, u32[]{:S(2)}, u32[]{:S(2)}) collective-permute-start(f32[264,128]{1,0:T(8,128)S(1)} %get-tuple-element.16.refs_2_), channel_id=1, source_target_pairs={{16,24},{20,28}} | collective-permute-start | bytes 405512 | tf_op jit(solution)/shard_map/ppermute | solution.py:120
  28.1 1.3 %collective-permute-start.13 = (f32[264,128]{1,0:T(8,128)S(1)}, f32[264,128]{1,0:T(8,128)}, u32[]{:S(2)}, u32[]{:S(2)}) collective-permute-start(f32[264,128]{1,0:T(8,128)S(1)} %get-tuple-element.16.refs_2_), channel_id=1, source_target_pairs={{25,24},{29,28}} | collective-permute-start | bytes 405512 | tf_op jit(solution)/shard_map/ppermute | solution.py:120
  29.5 1.0 %copy-done.5 = f32[8,128,128]{2,1,0:T(8,128)S(1)} copy-done((f32[8,128,128]{2,1,0:T(8,128)S(1)}, f32[8,128,128]{2,1,0:T(8,128)}, u32[]{:S(2)}) %copy-start.5) | copy-done | bytes 524312
  30.6 0.9 %copy-done.9 = f32[2,8,32,128]{3,2,1,0:T(8,128)S(1)} copy-done((f32[2,8,32,128]{3,2,1,0:T(8,128)S(1)}, f32[2,8,32,128]{3,2,1,0:T(8,128)}, u32[]{:S(2)}) %copy-start.9) | copy-done | bytes 262168
  31.5 1.9 %shard_map.49 = (f32[264,128]{1,0:T(8,128)}, f32[2,8,32,128]{3,2,1,0:T(8,128)S(1)}) custom-call(s32[3]{0:T(128)S(1)} %add_add_fusion.1.info, s32[2,8]{1,0:T(2,128)S(1)} %pad_add_fusion.up, f32[264,128]{1,0:T(8,128)} %collective-permute-done.12.refs_0_, f32[264,128]{1,0:T(8,128)} %collective-permute-done.13.refs_1_, ...), custom_call_target="tpu_custom_call" | custom-call | tf_op jit(solution)/shard_map/pallas_call | solution.py:154
  33.4 0.7 copy-done.12
  34.2 1.3 %collective-permute-done.14 = f32[8,32,128]{2,1,0:T(8,128)S(1)} collective-permute-done((f32[8,32,128]{2,1,0:T(8,128)S(1)}, f32[8,32,128]{2,1,0:T(8,128)S(1)}, u32[]{:S(2)}, u32[]{:S(2)}) %collective-permute-start.14) | collective-permute-done | bytes 131104 | tf_op jit(solution)/shard_map/ppermute | solution.py:123
  35.5 0.9 %bitcast_add_fusion = f32[8,32,128]{2,1,0:T(8,128)S(1)} fusion(f32[8,32,128]{2,1,0:T(8,128)S(1)} %collective-permute-done.14, f32[2,8,32,128]{3,2,1,0:T(8,128)} %copy-done.12, s32[]{:T(128)S(6)} %select_n.72), kind=kLoop, calls=%fused_computation.1 | loop fusion | flops 32768 | bytes 393220 | tf_op jit(solution)/shard_map/add | solution.py:159
  36.5 0.7 collective-permute-start.15
  37.1 0.7 collective-permute-start.16
  37.8 1.3 %collective-permute-start.17 = (f32[8,32,128]{2,1,0:T(8,128)S(1)}, f32[8,32,128]{2,1,0:T(8,128)S(1)}, u32[]{:S(2)}, u32[]{:S(2)}) collective-permute-start(f32[8,32,128]{2,1,0:T(8,128)S(1)} %bitcast_add_fusion), channel_id=1, source_target_pairs={{0,3},{4,7},{8,11},{12,15},{16,19},{20,23},{24,27},{28,31}} | collective-permute-start | bytes 393224 | tf_op jit(solution)/shard_map/ppermute | solution.py:120
  39.1 35.8 %collective-permute-done.17 = f32[8,32,128]{2,1,0:T(8,128)S(1)} collective-permute-done((f32[8,32,128]{2,1,0:T(8,128)S(1)}, f32[8,32,128]{2,1,0:T(8,128)S(1)}, u32[]{:S(2)}, u32[]{:S(2)}) %collective-permute-start.17) | collective-permute-done | bytes 131104 | tf_op jit(solution)/shard_map/ppermute | solution.py:120
  74.9 0.7 add_add_fusion
  (56 shorter events, 2.9 us)
Async XLA Ops:
  0.0 10.5 %copy-start = (f32[8,2,128,128]{3,2,1,0:T(8,128)S(1)}, f32[8,2,128,128]{3,2,1,0:T(8,128)}, u32[]{:S(2)}) copy-start(f32[8,2,128,128]{3,2,1,0:T(8,128)} %refs_6_.3) | copy-start | bytes 3145732
  0.0 3.7 %collective-permute-start = (s32[8,2]{0,1:T(2,128)}, s32[8,2]{0,1:T(2,128)S(1)}, u32[]{:S(2)}, u32[]{:S(2)}) collective-permute-start(s32[8,2]{0,1:T(2,128)} %param.7), channel_id=1, source_target_pairs={{0,4},{4,0},{8,12},{12,8},{16,20},{20,16},{24,28},{28,24},{1,5},{5... | collective-permute-start | bytes 200 | tf_op jit(solution)/shard_map/ppermute | solution.py:123
  0.0 10.5 %collective-permute-start.2 = (f32[8,2,128,128]{3,2,1,0:T(8,128)}, f32[8,2,128,128]{3,2,1,0:T(8,128)S(1)}, u32[]{:S(2)}, u32[]{:S(2)}) collective-permute-start(f32[8,2,128,128]{3,2,1,0:T(8,128)} %refs_6_.3), channel_id=1, source_target_pairs={{0,4},{4,0},{8,12},{12,8},{16,20},{20,16},{24,28},{28,24},{1,5},{5... | collective-permute-start | bytes 3145736 | tf_op jit(solution)/shard_map/ppermute | solution.py:123
  0.5 10.0 %collective-permute-start.1 = (f32[8,128,128]{2,1,0:T(8,128)}, f32[8,128,128]{2,1,0:T(8,128)S(1)}, u32[]{:S(2)}, u32[]{:S(2)}) collective-permute-start(f32[8,128,128]{2,1,0:T(8,128)} %refs_4_.1), channel_id=1, source_target_pairs={{0,4},{4,0},{8,12},{12,8},{16,20},{20,16},{24,28},{28,24},{1,5},{5... | collective-permute-start | bytes 1572872 | tf_op jit(solution)/shard_map/ppermute | solution.py:123
  0.6 9.9 %collective-permute-start.3 = (f32[8,32,128]{2,1,0:T(8,128)}, f32[8,32,128]{2,1,0:T(8,128)S(1)}, u32[]{:S(2)}, u32[]{:S(2)}) collective-permute-start(f32[8,32,128]{2,1,0:T(8,128)} %refs_10_.1), channel_id=1, source_target_pairs={{0,4},{4,0},{8,12},{12,8},{16,20},{20,16},{24,28},{28,24},{1,5},{5... | collective-permute-start | bytes 393224 | tf_op jit(solution)/shard_map/ppermute | solution.py:123
  2.1 2.3 %collective-permute-start.7 = (f32[8,128,128]{2,1,0:T(8,128)S(1)}, f32[8,128,128]{2,1,0:T(8,128)}, u32[]{:S(2)}, u32[]{:S(2)}) collective-permute-start(f32[8,128,128]{2,1,0:T(8,128)S(1)} %slice_bitcast_fusion), channel_id=1, source_target_pairs={{13,12},{21,20},{22,21},{29,28},{30,29},{31,30}} | collective-permute-start | bytes 1572872 | tf_op jit(solution)/shard_map/ppermute | solution.py:120
  4.4 10.7 %collective-permute-start.8 = (f32[8,128,128]{2,1,0:T(8,128)}, f32[8,128,128]{2,1,0:T(8,128)S(1)}, u32[]{:S(2)}, u32[]{:S(2)}) collective-permute-start(f32[8,128,128]{2,1,0:T(8,128)} %collective-permute-done.7.refs_10_.refs_9_.refs_8_), channel_id=1, source_target_pairs={{0,4},{4,0},{8,12},{12,8},{16,20},{20,16},{24,28},{28,24},{1,5},{5... | collective-permute-start | bytes 1572872 | tf_op jit(solution)/shard_map/ppermute | solution.py:123
  10.5 1.0 %copy-start.1 = (f32[8,128,128]{2,1,0:T(8,128)S(1)}, f32[8,128,128]{2,1,0:T(8,128)}, u32[]{:S(2)}) copy-start(f32[8,128,128]{2,1,0:T(8,128)} %refs_4_.1) | copy-start | bytes 1572868
  11.5 0.9 %copy-start.6 = (f32[8,32,128]{2,1,0:T(8,128)S(1)}, f32[8,32,128]{2,1,0:T(8,128)}, u32[]{:S(2)}) copy-start(f32[8,32,128]{2,1,0:T(8,128)} %refs_10_.1) | copy-start | bytes 393220
  12.4 2.8 %copy-start.2 = (f32[8,128,128]{2,1,0:T(8,128)S(1)}, f32[8,128,128]{2,1,0:T(8,128)}, u32[]{:S(2)}) copy-start(f32[8,128,128]{2,1,0:T(8,128)} %refs_4_.1) | copy-start | bytes 1572868
  13.0 2.1 %collective-permute-start.4 = (f32[264,128]{1,0:T(8,128)S(1)}, f32[264,128]{1,0:T(8,128)S(1)}, u32[]{:S(2)}, u32[]{:S(2)}) collective-permute-start(f32[264,128]{1,0:T(8,128)S(1)} %get-tuple-element.12.refs_4_), channel_id=1, source_target_pairs={{0,8},{4,12}} | collective-permute-start | bytes 405512 | tf_op jit(solution)/shard_map/ppermute | solution.py:120
  13.7 1.5 %collective-permute-start.5 = (f32[264,128]{1,0:T(8,128)S(1)}, f32[264,128]{1,0:T(8,128)S(1)}, u32[]{:S(2)}, u32[]{:S(2)}) collective-permute-start(f32[264,128]{1,0:T(8,128)S(1)} %get-tuple-element.12.refs_4_), channel_id=1, source_target_pairs={{0,17},{4,21}} | collective-permute-start | bytes 405512 | tf_op jit(solution)/shard_map/ppermute | solution.py:120
  14.4 0.8 %collective-permute-start.6 = (f32[264,128]{1,0:T(8,128)S(1)}, f32[264,128]{1,0:T(8,128)S(1)}, u32[]{:S(2)}, u32[]{:S(2)}) collective-permute-start(f32[264,128]{1,0:T(8,128)S(1)} %get-tuple-element.12.refs_4_), channel_id=1, source_target_pairs={{0,26},{4,30}} | collective-permute-start | bytes 405512 | tf_op jit(solution)/shard_map/ppermute | solution.py:120
  15.2 1.4 %copy-start.3 = (f32[8,128,128]{2,1,0:T(8,128)}, f32[8,128,128]{2,1,0:T(8,128)S(1)}, u32[]{:S(2)}) copy-start(f32[8,128,128]{2,1,0:T(8,128)S(1)} %collective-permute-done.8.refs_11_.refs_10_.refs_9_) | copy-start | bytes 1572868
  15.2 6.7 %copy-start.7 = (f32[8,32,128]{2,1,0:T(8,128)S(1)}, f32[8,32,128]{2,1,0:T(8,128)}, u32[]{:S(2)}) copy-start(f32[8,32,128]{2,1,0:T(8,128)} %refs_10_.1) | copy-start | bytes 393220
  16.5 0.7 copy-start.10
  17.2 4.7 %collective-permute-start.10 = (f32[264,128]{1,0:T(8,128)S(1)}, f32[264,128]{1,0:T(8,128)}, u32[]{:S(2)}, u32[]{:S(2)}) collective-permute-start(f32[264,128]{1,0:T(8,128)S(1)} %get-tuple-element.14.refs_3_), channel_id=1, source_target_pairs={{8,25},{12,29}} | collective-permute-start | bytes 405512 | tf_op jit(solution)/shard_map/ppermute | solution.py:120
  18.6 3.3 %collective-permute-start.11 = (f32[264,128]{1,0:T(8,128)S(1)}, f32[264,128]{1,0:T(8,128)}, u32[]{:S(2)}, u32[]{:S(2)}) collective-permute-start(f32[264,128]{1,0:T(8,128)S(1)} %get-tuple-element.14.refs_3_), channel_id=1, source_target_pairs={{17,16},{21,20},{26,25},{30,29}} | collective-permute-start | bytes 405512 | tf_op jit(solution)/shard_map/ppermute | solution.py:120
  19.9 2.0 %collective-permute-start.9 = (f32[264,128]{1,0:T(8,128)S(1)}, f32[264,128]{1,0:T(8,128)}, u32[]{:S(2)}, u32[]{:S(2)}) collective-permute-start(f32[264,128]{1,0:T(8,128)S(1)} %get-tuple-element.14.refs_3_), channel_id=1, source_target_pairs={{8,16},{12,20}} | collective-permute-start | bytes 405512 | tf_op jit(solution)/shard_map/ppermute | solution.py:120
  21.9 1.0 %copy-start.4 = (f32[8,128,128]{2,1,0:T(8,128)S(1)}, f32[8,128,128]{2,1,0:T(8,128)}, u32[]{:S(2)}) copy-start(f32[8,128,128]{2,1,0:T(8,128)} %copy-done.3) | copy-start | bytes 1572868
  23.0 0.9 %copy-start.11 = (f32[2,8,32,128]{3,2,1,0:T(8,128)S(1)}, f32[2,8,32,128]{3,2,1,0:T(8,128)}, u32[]{:S(2)}) copy-start(f32[2,8,32,128]{3,2,1,0:T(8,128)} %copy-done.10) | copy-start | bytes 786436
  23.9 0.9 %copy-start.14 = (f32[264,128]{1,0:T(8,128)S(1)}, f32[264,128]{1,0:T(8,128)}, u32[]{:S(2)}) copy-start(f32[264,128]{1,0:T(8,128)} %copy-done.13) | copy-start | bytes 405508
  26.1 0.7 copy-start.8
  26.8 2.7 %collective-permute-start.12 = (f32[264,128]{1,0:T(8,128)S(1)}, f32[264,128]{1,0:T(8,128)}, u32[]{:S(2)}, u32[]{:S(2)}) collective-permute-start(f32[264,128]{1,0:T(8,128)S(1)} %get-tuple-element.16.refs_2_), channel_id=1, source_target_pairs={{16,24},{20,28}} | collective-permute-start | bytes 405512 | tf_op jit(solution)/shard_map/ppermute | solution.py:120
  28.1 1.4 %collective-permute-start.13 = (f32[264,128]{1,0:T(8,128)S(1)}, f32[264,128]{1,0:T(8,128)}, u32[]{:S(2)}, u32[]{:S(2)}) collective-permute-start(f32[264,128]{1,0:T(8,128)S(1)} %get-tuple-element.16.refs_2_), channel_id=1, source_target_pairs={{25,24},{29,28}} | collective-permute-start | bytes 405512 | tf_op jit(solution)/shard_map/ppermute | solution.py:120
  29.5 1.0 %copy-start.5 = (f32[8,128,128]{2,1,0:T(8,128)S(1)}, f32[8,128,128]{2,1,0:T(8,128)}, u32[]{:S(2)}) copy-start(f32[8,128,128]{2,1,0:T(8,128)} %copy-done.3) | copy-start | bytes 1572868
  30.6 0.9 %copy-start.9 = (f32[2,8,32,128]{3,2,1,0:T(8,128)S(1)}, f32[2,8,32,128]{3,2,1,0:T(8,128)}, u32[]{:S(2)}) copy-start(f32[2,8,32,128]{3,2,1,0:T(8,128)} %copy-done.8) | copy-start | bytes 786436
  33.4 0.7 copy-start.12
  34.1 1.4 %collective-permute-start.14 = (f32[8,32,128]{2,1,0:T(8,128)S(1)}, f32[8,32,128]{2,1,0:T(8,128)S(1)}, u32[]{:S(2)}, u32[]{:S(2)}) collective-permute-start(f32[8,32,128]{2,1,0:T(8,128)S(1)} %dynamic-slice_bitcast_fusion), channel_id=1, source_target_pairs={{0,4},{4,0},{8,12},{12,8},{16,20},{20,16},{24,28},{28,24},{1,5},{5... | collective-permute-start | bytes 393224 | tf_op jit(solution)/shard_map/ppermute | solution.py:123
  36.5 2.7 %collective-permute-start.15 = (f32[8,32,128]{2,1,0:T(8,128)S(1)}, f32[8,32,128]{2,1,0:T(8,128)S(1)}, u32[]{:S(2)}, u32[]{:S(2)}) collective-permute-start(f32[8,32,128]{2,1,0:T(8,128)S(1)} %bitcast_add_fusion), channel_id=1, source_target_pairs={{0,1},{4,5},{8,9},{12,13},{16,17},{20,21},{24,25},{28,29}} | collective-permute-start | bytes 393224 | tf_op jit(solution)/shard_map/ppermute | solution.py:120
  37.1 2.0 %collective-permute-start.16 = (f32[8,32,128]{2,1,0:T(8,128)S(1)}, f32[8,32,128]{2,1,0:T(8,128)S(1)}, u32[]{:S(2)}, u32[]{:S(2)}) collective-permute-start(f32[8,32,128]{2,1,0:T(8,128)S(1)} %bitcast_add_fusion), channel_id=1, source_target_pairs={{0,2},{4,6},{8,10},{12,14},{16,18},{20,22},{24,26},{28,30}} | collective-permute-start | bytes 393224 | tf_op jit(solution)/shard_map/ppermute | solution.py:120
  37.8 37.1 %collective-permute-start.17 = (f32[8,32,128]{2,1,0:T(8,128)S(1)}, f32[8,32,128]{2,1,0:T(8,128)S(1)}, u32[]{:S(2)}, u32[]{:S(2)}) collective-permute-start(f32[8,32,128]{2,1,0:T(8,128)S(1)} %bitcast_add_fusion), channel_id=1, source_target_pairs={{0,3},{4,7},{8,11},{12,15},{16,19},{20,23},{24,27},{28,31}} | collective-permute-start | bytes 393224 | tf_op jit(solution)/shard_map/ppermute | solution.py:120
  (2 other events, 1.3 us)

commit v2 on v0

v2 whole, which is shorter than its diff:
```python
import functools

import jax
import jax.numpy as jnp
from jax import lax
from jax.experimental import pallas as pl
from jax.experimental.pallas import tpu as pltpu
from jax.sharding import PartitionSpec as P


F32 = jnp.float32
BF16 = jnp.bfloat16
I32 = jnp.int32


def position():
    level = lax.axis_index("level")
    return lax.rem(level, 2), lax.div(level, 2), lax.axis_index("row")


def split(v):
    high = v.astype(BF16)
    return high, (v - high.astype(F32)).astype(BF16)


def product(xs, ws, transposed=False):
    dims = (((1,), (1 if transposed else 0,)), ((), ()))
    parts = [(split(x), split(w)) for x, w in zip(xs, ws)]
    mul = lambda x, w: lax.dot_general(x, w, dims, preferred_element_type=F32)
    out = []
    for (xh, xl), (wh, wl) in parts:
        both = mul(jnp.concatenate([xh, xl], 0), wh)
        rows = xh.shape[0]
        out.append(both[:rows] + both[rows:] + mul(xh, wl))
    return out


def plus(xs, ys):
    return [x + y for x, y in zip(xs, ys)]


def emit(half, rows, msg, tb, xa, xb):
    for i in range(half):
        msg[pl.ds(i * rows, rows), :] = xa[i]
        msg[pl.ds((half + i) * rows, rows), :] = xb[i]
        msg[pl.ds(2 * half * rows + i, 1), :] = jnp.full((1, xa[i].shape[1]), tb[i], I32).astype(F32)


def load_kernel(n, rows, inv_h, blk_h, rhs_h, inv, blk, rhs, first, x0, sems):
    member, stage, _ = position()
    copies = [
        pltpu.make_async_copy(inv_h, inv, sems.at[0]),
        pltpu.make_async_copy(rhs_h, rhs, sems.at[1]),
        pltpu.make_async_copy(blk_h, blk, sems.at[2]),
    ]
    for copy in copies:
        copy.start()
    copies[0].wait()
    copies[1].wait()

    @pl.when(jnp.logical_and(stage == 0, member == 0))
    def _():
        for i, x in enumerate(product([rhs[t] for t in range(n)], [inv[t] for t in range(n)], True)):
            x0[pl.ds(i * rows, rows), :] = x

    copies[2].wait()
    for t in range(n):
        first[t] = blk[t, 0]


def scatter(n, source, column, maps, row):
    for t in range(n):
        maps[row, t] = 0
    for t in range(n):
        @pl.when(source[column, t] >= 0)
        def _():
            maps[row, lax.rem(source[column, t], n)] = t


def early_kernel(n, half, rows, own, x0, blk, low, high, place):
    member, stage, plane = position()

    @pl.when(jnp.logical_and(member == 1, stage == plane))
    def _():
        scatter(n, own, 0, place, 0)
        us = product([x0[pl.ds(k * rows, rows), :] for k in range(n)], [blk[place[0, k], 0] for k in range(n)])
        for i in range(half):
            low[pl.ds(i * rows, rows), :] = us[i]
            high[pl.ds(i * rows, rows), :] = us[half + i]


def first_kernel(n, half, rows, own, oth, inv0, inv1, blk0, blk1, rhs0, rhs1, msg, maps):
    member, stage, plane = position()
    active = jnp.logical_and(stage == 0, plane == 0)

    def run(src_b, inv_a, inv_b, blk_b, rhs_a, rhs_b):
        scatter(n, src_b, 0, maps, 0)
        ta = [member * half + i for i in range(half)]
        tb = [maps[0, t] for t in ta]
        xa = product([rhs_a[t] for t in ta], [inv_a[t] for t in ta], True)
        ub = product(xa, [blk_b[t, 0] for t in tb])
        xb = product([rhs_b[t] - u for t, u in zip(tb, ub)], [inv_b[t] for t in tb], True)
        msg[pl.ds(2 * half * rows, 8), :] = jnp.zeros((8, msg.shape[1]), F32)
        emit(half, rows, msg, tb, xa, xb)

    @pl.when(jnp.logical_not(active))
    def _():
        msg[...] = jnp.zeros_like(msg)

    @pl.when(jnp.logical_and(active, member == 0))
    def _():
        run(oth, inv0, inv1, blk1, rhs0, rhs1)

    @pl.when(jnp.logical_and(active, member == 1))
    def _():
        run(own, inv1, inv0, blk0, rhs1, rhs0)


def step_kernel(n, half, rows, g, count, last, own, oth, *refs):
    refs, maps = refs[:-1], refs[-1]
    member, stage, plane = position()
    active, solver = stage - 1 - plane == g, plane == 0
    xs = refs[:count]
    more = refs[count:count + 2]
    msg_in, inv0, inv1, blk0, blk1, rhs0, rhs1 = refs[count + 2:count + 9]
    rest = refs[count + 9:]
    if g:
        acc, (pre0, pre1), rest = more[0], (more[1], rest[0]), rest[1:]
    else:
        pre0 = pre1 = None
    msg, outs = (rest[2], rest[:2]) if last else (rest[0], None)

    @pl.when(jnp.logical_not(active))
    def _():
        msg[...] = msg_in[...]

    def arrived(start, size):
        total = xs[0][pl.ds(start, size), :]
        for x in xs[1:]:
            total = total + x[pl.ds(start, size), :]
        return total

    def run(src_a, src_b, inv_a, inv_b, blk_a, blk_b, pre, rhs_a, rhs_b):
        scatter(n, src_a, 0, maps, 0)
        scatter(n, src_b, 1, maps, 1)
        ids = arrived(2 * half * rows, 8)
        child = [jnp.max(ids[i:i + 1]).astype(I32) for i in range(half)]
        ta, tb = [maps[0, c] for c in child], [maps[1, c] for c in child]
        sa = [arrived(i * rows, rows) for i in range(half)]
        sb = [arrived((half + i) * rows, rows) for i in range(half)]
        ua = plus(product(sa, [blk_a[t, 1] for t in ta]), product(sb, [blk_a[t, 0] for t in ta]))
        ub = product(sb, [blk_b[t, 1] for t in tb])
        if g:
            ua = plus(ua, [acc[pl.ds(i * rows, rows), :] for i in range(half)])
            ub = plus(ub, [acc[pl.ds((half + i) * rows, rows), :] for i in range(half)])
            ub = plus(ub, product(sa, [pre[t] for t in tb]))
        else:
            ub = plus(ub, [more[0][pl.ds(i * rows, rows), :] + more[1][pl.ds(i * rows, rows), :] for i in range(half)])
        msg[pl.ds(2 * half * rows, 8), :] = jnp.zeros((8, msg.shape[1]), F32)

        @pl.when(solver)
        def _():
            xa = product([rhs_a[t] - u for t, u in zip(ta, ua)], [inv_a[t] for t in ta], True)
            vb = plus(ub, product(xa, [blk_b[t, 0] for t in tb]))
            xb = product([rhs_b[t] - v for t, v in zip(tb, vb)], [inv_b[t] for t in tb], True)
            emit(half, rows, msg, tb, xa, xb)

        @pl.when(jnp.logical_not(solver))
        def _():
            emit(half, rows, msg, [0] * half, ua, ub)

    @pl.when(jnp.logical_and(active, member == 0))
    def _():
        run(own, oth, inv0, inv1, blk0, blk1, pre1, rhs0, rhs1)

    @pl.when(jnp.logical_and(active, member == 1))
    def _():
        run(oth, own, inv1, inv0, blk1, blk0, pre0, rhs1, rhs0)

    if last:
        mine, theirs = outs
        mine[...] = jnp.zeros_like(mine)
        theirs[...] = jnp.zeros_like(theirs)

        def place(src_b, out_a, out_b):
            ids = msg[pl.ds(2 * half * rows, 8), :]
            for i in range(half):
                tb = jnp.max(ids[i:i + 1]).astype(I32)
                out_a[lax.rem(jnp.maximum(src_b[0, tb], 0), n)] = msg[pl.ds(i * rows, rows), :]
                out_b[tb] = msg[pl.ds((half + i) * rows, rows), :]

        @pl.when(jnp.logical_and(solver, member == 0))
        def _():
            place(oth, mine, theirs)

        @pl.when(jnp.logical_and(solver, member == 1))
        def _():
            place(own, theirs, mine)


def pick_kernel(*refs):
    _, _, plane = position()
    zs, out, sem = refs[:-2], refs[-2], refs[-1]
    for q, z in enumerate(zs):
        @pl.when(plane == q)
        def _():
            copy = pltpu.make_async_copy(z, out, sem)
            copy.start()
            copy.wait()


SMEM, VMEM, HBM = pltpu.SMEM, pltpu.VMEM, pltpu.HBM


def call(kernel, ins, outs, shapes, scratch=()):
    def run(*args):
        args = [pltpu.with_memory_space_constraint(a, m) if m in (VMEM, HBM) else a for a, m in zip(args, ins)]
        return run_raw(*args)

    run_raw = pl.pallas_call(
        kernel,
        out_shape=shapes,
        in_specs=[pl.BlockSpec(memory_space=s) for s in ins],
        out_specs=[pl.BlockSpec(memory_space=s) for s in outs],
        scratch_shapes=scratch,
        compiler_params=pltpu.CompilerParams(vmem_limit_bytes=4 * 1024 * 1024),
    )
    return run


def solve(right_side, inverses, blocks, sources):
    n, rows, w = right_side.shape
    half = n // 2
    levels, planes = lax.axis_size("level"), lax.axis_size("row")
    stages = levels // 2
    shape = lambda *s: jax.ShapeDtypeStruct(s, F32)

    def move(value, pairs):
        return lax.ppermute(value, ("level", "row"), [(a * planes + b, c * planes + d) for (a, b), (c, d) in pairs])

    def other(value):
        return lax.ppermute(value, "level", [(i, i ^ 1) for i in range(levels)])

    own = sources.T
    oth = other(own)
    inv_o, rhs_o, blk_o = other(inverses), other(right_side), other(blocks)

    inv, blk, rhs, first, x0 = call(
        functools.partial(load_kernel, n, rows), [HBM] * 3, [VMEM] * 5,
        [shape(n, w, w), shape(n, 2, w, w), shape(n, rows, w), shape(n, w, w), shape(n * rows, w)], [pltpu.SemaphoreType.DMA((3,))],
    )(inverses, blocks, right_side)
    x0 = move(x0, [((0, h), (2 * h + 1, h)) for h in range(1, stages)])
    pre = move(first, [((2 * h + 1, p + 1), (2 * h + 1, p)) for h in range(2, stages) for p in range(h - 1)])

    msg_shape = shape(2 * half * rows + 8, w)
    msg, = call(functools.partial(first_kernel, n, half, rows), [SMEM] * 2 + [VMEM] * 6, [VMEM], [msg_shape], [pltpu.SMEM((1, n), I32)])(
        own, oth, inv, inv_o, blk, blk_o, rhs, rhs_o)
    early = call(functools.partial(early_kernel, n, half, rows), [SMEM] + [VMEM] * 2, [VMEM] * 2, [shape(half * rows, w)] * 2, [pltpu.SMEM((1, n), I32)])(own, x0, blk)
    early = [move(early[m], [((2 * h + 1, h), (2 * h + m, h - 1)) for h in range(1, stages)]) for m in (0, 1)]

    for g in range(stages - 1):
        xs = [move(msg, [((2 * g + m, 0), (2 * (g + d) + m, d - 1)) for m in (0, 1)]) for d in range(1, stages - g)]
        if g:
            acc = move(msg, [((2 * h + m, h - g), (2 * h + m, h - g - 1)) for h in range(g + 1, stages) for m in (0, 1)])
        if g == 1:
            pre_o = other(pre)
        last = g == stages - 2
        more, after = ([acc, pre], [pre_o]) if g else (early, [])
        outs = [shape(n, rows, w)] * 2 if last else [msg_shape]
        scratch = ([pltpu.VMEM(msg_shape.shape, F32)] if last else []) + [pltpu.SMEM((2, n), I32)]
        got = call(functools.partial(step_kernel, n, half, rows, g, len(xs), last), [SMEM] * 2 + [VMEM] * (len(xs) + 9 + len(after)), [VMEM] * len(outs), outs, scratch)(
            own, oth, *xs, *more, msg, inv, inv_o, blk, blk_o, rhs, rhs_o, *after)
        msg = got[0]

    mine, theirs = got
    solved = mine + other(theirs)
    zs = [solved] + [move(solved, [((l, 0), (l, q)) for l in range(levels)]) for q in range(1, planes)]
    out, = call(pick_kernel, [VMEM] * planes, [HBM], [shape(n, rows, w)], [pltpu.SemaphoreType.DMA])(
        *zs)
    return out


def solution(mesh):
    return jax.shard_map(
        solve,
        mesh=mesh,
        in_specs=(
            P("level", None, None),
            P("level", None, None),
            P("level", "row", None, None),
            P("level", "row"),
        ),
        out_specs=P("level", None, None),
        check_vma=False,
    )
```

time: 782 us -> 58.7 us (0.08)
  the two profiles are of different devices: /device:TPU:30 before, /device:TPU:14 now
where the time goes in v2:
time: 58.7 us; the launch traced here: 58.4 us
  waiting for transfers between devices  29.6 us (50%)
  starting transfers between devices  22.8 us (39%)
  Pallas kernels  5.72 us (10%)
    ppermute x15, waiting for transfers between devices, move(): lax.ppermute(value, ('level', 'row'), [(a * planes + b, c * planes + d) f...  27 us
    ppermute x15, starting transfers between devices, move(): lax.ppermute(value, ('level', 'row'), [(a * planes + b, c * planes + d) f...  12.5 us
    ppermute x6, starting transfers between devices, other(): return lax.ppermute(value, 'level', [(i, i ^ 1) for i in range(levels)])  10.2 us
    pallas_call x7, Pallas kernels, run(): return run_raw(*args)  5.72 us
    ppermute x6, waiting for transfers between devices, other(): return lax.ppermute(value, 'level', [(i, i ^ 1) for i in range(levels)])  2.55 us
  transfers between devices with their start and end apart: 21, of which 6 were waited for; matrix products, arithmetic and copies ran while one was open for 0% of the time, Pallas kernels for 6%

profile of v2, /device:TPU:14, one launch (start us, length us, event | category | flops | bytes accessed | tf_op | source)
XLA Modules:
  0.0 58.4 jit_solution(17918929712136993851)
XLA Ops:
  0.0 1.5 %shard_map.46 = (f32[8,128,128]{2,1,0:T(8,128)S(1)}, f32[8,2,128,128]{3,2,1,0:T(8,128)S(1)}, f32[8,32,128]{2,1,0:T(8,128)S(1)}, f32[8,128,128]{2,1,0:T(8,128)S(1)}, f32[256,128]{1,0:T(8,128)S(1)}) custom-call(f32[8,128,128]{2,1,0:T(8,128)} %inv_h.1, f32[8,2,128,128]{3,2,1,0:T(8,128)} %blk_h.1, f32[8,32,128]{2,1,0:T(8,128)} %rhs_h.1), custom_call_target="tpu_custom_call" | custom-call | tf_op jit(solution)/shard_map/pallas_call | solution.py:218
  1.6 0.7 %collective-permute-start.13 = (f32[8,128,128]{2,1,0:T(8,128)S(1)}, f32[8,128,128]{2,1,0:T(8,128)S(1)}, u32[]{:S(2)}, u32[]{:S(2)}) collective-permute-start(f32[8,128,128]{2,1,0:T(8,128)S(1)} %get-tuple-element.20), channel_id=1, source_target_pairs={{21,20},{29,28},{30,29}} | collective-permute-start | bytes 1572872 | tf_op jit(solution)/shard_map/ppermute | solution.py:239
  2.3 1.9 %collective-permute-start.1 = (f32[8,128,128]{2,1,0:T(8,128)S(1)}, f32[8,128,128]{2,1,0:T(8,128)S(1)}, u32[]{:S(2)}, u32[]{:S(2)}) collective-permute-start(f32[8,128,128]{2,1,0:T(8,128)S(1)} %copy-done.1), channel_id=1, source_target_pairs={{0,4},{4,0},{8,12},{12,8},{16,20},{20,16},{24,28},{28,24},{1,5},{5... | collective-permute-start | bytes 1572872 | tf_op jit(solution)/shard_map/ppermute | solution.py:242
  4.2 7.8 %collective-permute-start.14 = (f32[8,128,128]{2,1,0:T(8,128)S(1)}, f32[8,128,128]{2,1,0:T(8,128)S(1)}, u32[]{:S(2)}, u32[]{:S(2)}) collective-permute-start(f32[8,128,128]{2,1,0:T(8,128)S(1)} %collective-permute-done.13.refs_3_.refs_2_), channel_id=1, source_target_pairs={{0,4},{4,0},{8,12},{12,8},{16,20},{20,16},{24,28},{28,24},{1,5},{5... | collective-permute-start | bytes 1572872 | tf_op jit(solution)/shard_map/ppermute | solution.py:242
  12.0 0.5 collective-permute-start
  12.5 1.2 %collective-permute-done.oth = s32[2,8]{1,0:T(2,128)S(1)} collective-permute-done((s32[2,8]{1,0:T(2,128)S(1)}, s32[2,8]{1,0:T(2,128)S(1)}, u32[]{:S(2)}, u32[]{:S(2)}) %collective-permute-start) | collective-permute-done | bytes 96 | tf_op jit(solution)/shard_map/ppermute | solution.py:242
  13.7 0.7 %collective-permute-start.7 = (f32[256,128]{1,0:T(8,128)S(1)}, f32[256,128]{1,0:T(8,128)S(1)}, u32[]{:S(2)}, u32[]{:S(2)}) collective-permute-start(f32[256,128]{1,0:T(8,128)S(1)} %get-tuple-element.17), channel_id=1, source_target_pairs={{1,13},{2,22},{3,31}} | collective-permute-start | bytes 393224 | tf_op jit(solution)/shard_map/ppermute | solution.py:239
  14.4 0.6 %shard_map.47.refs_5_ = f32[264,128]{1,0:T(8,128)S(1)} custom-call(s32[2,8]{1,0:T(2,128)S(1)} %bitcast.2, s32[2,8]{1,0:T(2,128)S(1)} %collective-permute-done.oth, f32[8,128,128]{2,1,0:T(8,128)S(1)} %get-tuple-element.14.inv0.refs_6_.refs_5_.refs_4_, f32[8,128,128]{2,1,0:T(8,128)S(1)} %collective-permute-done.1.inv1.refs_7_.refs_6_.refs_5_, ...), custom_call_target="tpu_custom_call" | custom-call | tf_op jit(solution)/shard_map/pallas_call | solution.py:218
  15.0 0.7 %collective-permute-start.6 = (f32[264,128]{1,0:T(8,128)S(1)}, f32[264,128]{1,0:T(8,128)S(1)}, u32[]{:S(2)}, u32[]{:S(2)}) collective-permute-start(f32[264,128]{1,0:T(8,128)S(1)} %shard_map.47.refs_5_), channel_id=1, source_target_pairs={{0,26},{4,30}} | collective-permute-start | bytes 405512 | tf_op jit(solution)/shard_map/ppermute | solution.py:239
  15.7 0.7 %collective-permute-start.5 = (f32[264,128]{1,0:T(8,128)S(1)}, f32[264,128]{1,0:T(8,128)S(1)}, u32[]{:S(2)}, u32[]{:S(2)}) collective-permute-start(f32[264,128]{1,0:T(8,128)S(1)} %shard_map.47.refs_5_), channel_id=1, source_target_pairs={{0,17},{4,21}} | collective-permute-start | bytes 405512 | tf_op jit(solution)/shard_map/ppermute | solution.py:239
  16.3 0.7 %collective-permute-start.4 = (f32[264,128]{1,0:T(8,128)S(1)}, f32[264,128]{1,0:T(8,128)S(1)}, u32[]{:S(2)}, u32[]{:S(2)}) collective-permute-start(f32[264,128]{1,0:T(8,128)S(1)} %shard_map.47.refs_5_), channel_id=1, source_target_pairs={{0,8},{4,12}} | collective-permute-start | bytes 405512 | tf_op jit(solution)/shard_map/ppermute | solution.py:239
  17.0 0.6 shard_map.48
  17.6 0.7 %collective-permute-start.8 = (f32[128,128]{1,0:T(8,128)S(1)}, f32[128,128]{1,0:T(8,128)S(1)}, u32[]{:S(2)}, u32[]{:S(2)}) collective-permute-start(f32[128,128]{1,0:T(8,128)S(1)} %get-tuple-element.18), channel_id=1, source_target_pairs={{13,8},{22,17},{31,26}} | collective-permute-start | bytes 196616 | tf_op jit(solution)/shard_map/ppermute | solution.py:239
  18.3 0.7 %collective-permute-start.9 = (f32[128,128]{1,0:T(8,128)S(1)}, f32[128,128]{1,0:T(8,128)S(1)}, u32[]{:S(2)}, u32[]{:S(2)}) collective-permute-start(f32[128,128]{1,0:T(8,128)S(1)} %get-tuple-element.19), channel_id=1, source_target_pairs={{13,12},{22,21},{31,30}} | collective-permute-start | bytes 196616 | tf_op jit(solution)/shard_map/ppermute | solution.py:239
  19.0 0.6 %shard_map.49.refs_4_ = f32[264,128]{1,0:T(8,128)S(1)} custom-call(s32[2,8]{1,0:T(2,128)S(1)} %bitcast.4, s32[2,8]{1,0:T(2,128)S(1)} %collective-permute-done.oth, f32[264,128]{1,0:T(8,128)S(1)} %collective-permute-done.4.refs_0_, f32[264,128]{1,0:T(8,128)S(1)} %collective-permute-done.5.refs_1_, f32[264,128]{1,0:T(8,128)S(1)} %collective-permute-done.6.refs_2_, ...), custom_call_target="tpu_custom_call" | custom-call | tf_op jit(solution)/shard_map/pallas_call | solution.py:218
  19.6 1.3 %collective-permute-start.12 = (f32[264,128]{1,0:T(8,128)S(1)}, f32[264,128]{1,0:T(8,128)S(1)}, u32[]{:S(2)}, u32[]{:S(2)}) collective-permute-start(f32[264,128]{1,0:T(8,128)S(1)} %shard_map.49.refs_4_), channel_id=1, source_target_pairs={{17,16},{21,20},{26,25},{30,29}} | collective-permute-start | bytes 405512 | tf_op jit(solution)/shard_map/ppermute | solution.py:239
  20.9 1.3 %collective-permute-start.11 = (f32[264,128]{1,0:T(8,128)S(1)}, f32[264,128]{1,0:T(8,128)S(1)}, u32[]{:S(2)}, u32[]{:S(2)}) collective-permute-start(f32[264,128]{1,0:T(8,128)S(1)} %shard_map.49.refs_4_), channel_id=1, source_target_pairs={{8,25},{12,29}} | collective-permute-start | bytes 405512 | tf_op jit(solution)/shard_map/ppermute | solution.py:239
  22.2 0.7 %collective-permute-start.10 = (f32[264,128]{1,0:T(8,128)S(1)}, f32[264,128]{1,0:T(8,128)S(1)}, u32[]{:S(2)}, u32[]{:S(2)}) collective-permute-start(f32[264,128]{1,0:T(8,128)S(1)} %shard_map.49.refs_4_), channel_id=1, source_target_pairs={{8,16},{12,20}} | collective-permute-start | bytes 405512 | tf_op jit(solution)/shard_map/ppermute | solution.py:239
  22.9 9.3 %collective-permute-done.12.refs_2_ = f32[264,128]{1,0:T(8,128)S(1)} collective-permute-done((f32[264,128]{1,0:T(8,128)S(1)}, f32[264,128]{1,0:T(8,128)S(1)}, u32[]{:S(2)}, u32[]{:S(2)}) %collective-permute-start.12) | collective-permute-done | bytes 135200 | tf_op jit(solution)/shard_map/ppermute | solution.py:239
  32.2 1.6 %collective-permute-done.11.refs_1_ = f32[264,128]{1,0:T(8,128)S(1)} collective-permute-done((f32[264,128]{1,0:T(8,128)S(1)}, f32[264,128]{1,0:T(8,128)S(1)}, u32[]{:S(2)}, u32[]{:S(2)}) %collective-permute-start.11) | collective-permute-done | bytes 135200 | tf_op jit(solution)/shard_map/ppermute | solution.py:239
  33.8 1.1 %shard_map.50.refs_3_ = f32[264,128]{1,0:T(8,128)S(1)} custom-call(s32[2,8]{1,0:T(2,128)S(1)} %bitcast.5, s32[2,8]{1,0:T(2,128)S(1)} %collective-permute-done.oth, f32[264,128]{1,0:T(8,128)S(1)} %collective-permute-done.10.refs_0_, f32[264,128]{1,0:T(8,128)S(1)} %collective-permute-done.11.refs_1_, f32[264,128]{1,0:T(8,128)S(1)} %collective-permute-done.12.refs_2_, ...), custom_call_target="tpu_custom_call" | custom-call | tf_op jit(solution)/shard_map/pallas_call | solution.py:218
  35.0 1.3 %collective-permute-start.16 = (f32[264,128]{1,0:T(8,128)S(1)}, f32[264,128]{1,0:T(8,128)S(1)}, u32[]{:S(2)}, u32[]{:S(2)}) collective-permute-start(f32[264,128]{1,0:T(8,128)S(1)} %shard_map.50.refs_3_), channel_id=1, source_target_pairs={{25,24},{29,28}} | collective-permute-start | bytes 405512 | tf_op jit(solution)/shard_map/ppermute | solution.py:239
  36.3 0.7 %collective-permute-start.15 = (f32[264,128]{1,0:T(8,128)S(1)}, f32[264,128]{1,0:T(8,128)S(1)}, u32[]{:S(2)}, u32[]{:S(2)}) collective-permute-start(f32[264,128]{1,0:T(8,128)S(1)} %shard_map.50.refs_3_), channel_id=1, source_target_pairs={{16,24},{20,28}} | collective-permute-start | bytes 405512 | tf_op jit(solution)/shard_map/ppermute | solution.py:239
  36.9 1.9 %collective-permute-done.16.refs_1_ = f32[264,128]{1,0:T(8,128)S(1)} collective-permute-done((f32[264,128]{1,0:T(8,128)S(1)}, f32[264,128]{1,0:T(8,128)S(1)}, u32[]{:S(2)}, u32[]{:S(2)}) %collective-permute-start.16) | collective-permute-done | bytes 135200 | tf_op jit(solution)/shard_map/ppermute | solution.py:239
  38.8 0.6 %shard_map.51 = (f32[8,32,128]{2,1,0:T(8,128)S(1)}, f32[8,32,128]{2,1,0:T(8,128)S(1)}) custom-call(s32[2,8]{1,0:T(2,128)S(1)} %bitcast.6, s32[2,8]{1,0:T(2,128)S(1)} %collective-permute-done.oth, f32[264,128]{1,0:T(8,128)S(1)} %collective-permute-done.15.refs_0_, f32[264,128]{1,0:T(8,128)S(1)} %collective-permute-done.16.refs_1_, ...), custom_call_target="tpu_custom_call" | custom-call | tf_op jit(solution)/shard_map/pallas_call | solution.py:218
  39.4 0.1 collective-permute-start.17
  39.5 1.3 %collective-permute-done.17 = f32[8,32,128]{2,1,0:T(8,128)S(1)} collective-permute-done((f32[8,32,128]{2,1,0:T(8,128)S(1)}, f32[8,32,128]{2,1,0:T(8,128)S(1)}, u32[]{:S(2)}, u32[]{:S(2)}) %collective-permute-start.17) | collective-permute-done | bytes 131104 | tf_op jit(solution)/shard_map/ppermute | solution.py:242
  40.9 0.7 %collective-permute-start.20 = (f32[8,32,128]{2,1,0:T(8,128)S(1)}, f32[8,32,128]{2,1,0:T(8,128)S(1)}, u32[]{:S(2)}, u32[]{:S(2)}) collective-permute-start(f32[8,32,128]{2,1,0:T(8,128)S(1)} %add.3.refs_0_), channel_id=1, source_target_pairs={{0,3},{4,7},{8,11},{12,15},{16,19},{20,23},{24,27},{28,31}} | collective-permute-start | bytes 393224 | tf_op jit(solution)/shard_map/ppermute | solution.py:239
  41.5 0.7 %collective-permute-start.19 = (f32[8,32,128]{2,1,0:T(8,128)S(1)}, f32[8,32,128]{2,1,0:T(8,128)S(1)}, u32[]{:S(2)}, u32[]{:S(2)}) collective-permute-start(f32[8,32,128]{2,1,0:T(8,128)S(1)} %add.3.refs_0_), channel_id=1, source_target_pairs={{0,2},{4,6},{8,10},{12,14},{16,18},{20,22},{24,26},{28,30}} | collective-permute-start | bytes 393224 | tf_op jit(solution)/shard_map/ppermute | solution.py:239
  42.2 1.3 %collective-permute-start.18 = (f32[8,32,128]{2,1,0:T(8,128)S(1)}, f32[8,32,128]{2,1,0:T(8,128)S(1)}, u32[]{:S(2)}, u32[]{:S(2)}) collective-permute-start(f32[8,32,128]{2,1,0:T(8,128)S(1)} %add.3.refs_0_), channel_id=1, source_target_pairs={{0,1},{4,5},{8,9},{12,13},{16,17},{20,21},{24,25},{28,29}} | collective-permute-start | bytes 393224 | tf_op jit(solution)/shard_map/ppermute | solution.py:239
  43.5 14.2 %collective-permute-done.18.refs_1_ = f32[8,32,128]{2,1,0:T(8,128)S(1)} collective-permute-done((f32[8,32,128]{2,1,0:T(8,128)S(1)}, f32[8,32,128]{2,1,0:T(8,128)S(1)}, u32[]{:S(2)}, u32[]{:S(2)}) %collective-permute-start.18) | collective-permute-done | bytes 131104 | tf_op jit(solution)/shard_map/ppermute | solution.py:239
  57.7 0.7 %shard_map.52 = f32[8,32,128]{2,1,0:T(8,128)} custom-call(f32[8,32,128]{2,1,0:T(8,128)S(1)} %add.3.refs_0_, f32[8,32,128]{2,1,0:T(8,128)S(1)} %collective-permute-done.18.refs_1_, f32[8,32,128]{2,1,0:T(8,128)S(1)} %collective-permute-done.19.refs_2_, f32[8,32,128]{2,1,0:T(8,128)S(1)} %collective-permute-done.20.refs_3_), custom_call_target="tpu_custom_call" | custom-call | tf_op jit(solution)/shard_map/pallas_call | solution.py:218
  (24 shorter events, 0.1 us)
Async XLA Ops:
  0.0 2.3 %copy-start.1 = (f32[8,128,128]{2,1,0:T(8,128)S(1)}, f32[8,128,128]{2,1,0:T(8,128)}, u32[]{:S(2)}) copy-start(f32[8,128,128]{2,1,0:T(8,128)} %inv_h.1) | copy-start | bytes 1572868
  0.0 11.9 %copy-start.2 = (f32[8,32,128]{2,1,0:T(8,128)S(1)}, f32[8,32,128]{2,1,0:T(8,128)}, u32[]{:S(2)}) copy-start(f32[8,32,128]{2,1,0:T(8,128)} %rhs_h.1) | copy-start | bytes 393220
  0.0 14.4 %collective-permute-start.2 = (f32[8,2,128,128]{3,2,1,0:T(8,128)}, f32[8,2,128,128]{3,2,1,0:T(8,128)S(1)}, u32[]{:S(2)}, u32[]{:S(2)}) collective-permute-start(f32[8,2,128,128]{3,2,1,0:T(8,128)} %blk_h.1), channel_id=1, source_target_pairs={{0,4},{4,0},{8,12},{12,8},{16,20},{20,16},{24,28},{28,24},{1,5},{5... | collective-permute-start | bytes 3145736 | tf_op jit(solution)/shard_map/ppermute | solution.py:242
  1.6 10.4 %copy-start = (s32[8,2]{0,1:T(2,128)S(1)}, s32[8,2]{0,1:T(2,128)}, u32[]{:S(2)}) copy-start(s32[8,2]{0,1:T(2,128)} %param.7) | copy-start | bytes 196
  1.6 2.6 %collective-permute-start.13 = (f32[8,128,128]{2,1,0:T(8,128)S(1)}, f32[8,128,128]{2,1,0:T(8,128)S(1)}, u32[]{:S(2)}, u32[]{:S(2)}) collective-permute-start(f32[8,128,128]{2,1,0:T(8,128)S(1)} %get-tuple-element.20), channel_id=1, source_target_pairs={{21,20},{29,28},{30,29}} | collective-permute-start | bytes 1572872 | tf_op jit(solution)/shard_map/ppermute | solution.py:239
  2.3 12.1 %collective-permute-start.1 = (f32[8,128,128]{2,1,0:T(8,128)S(1)}, f32[8,128,128]{2,1,0:T(8,128)S(1)}, u32[]{:S(2)}, u32[]{:S(2)}) collective-permute-start(f32[8,128,128]{2,1,0:T(8,128)S(1)} %copy-done.1), channel_id=1, source_target_pairs={{0,4},{4,0},{8,12},{12,8},{16,20},{20,16},{24,28},{28,24},{1,5},{5... | collective-permute-start | bytes 1572872 | tf_op jit(solution)/shard_map/ppermute | solution.py:242
  4.2 18.7 %collective-permute-start.14 = (f32[8,128,128]{2,1,0:T(8,128)S(1)}, f32[8,128,128]{2,1,0:T(8,128)S(1)}, u32[]{:S(2)}, u32[]{:S(2)}) collective-permute-start(f32[8,128,128]{2,1,0:T(8,128)S(1)} %collective-permute-done.13.refs_3_.refs_2_), channel_id=1, source_target_pairs={{0,4},{4,0},{8,12},{12,8},{16,20},{20,16},{24,28},{28,24},{1,5},{5... | collective-permute-start | bytes 1572872 | tf_op jit(solution)/shard_map/ppermute | solution.py:242
  12.0 2.4 %collective-permute-start.3 = (f32[8,32,128]{2,1,0:T(8,128)S(1)}, f32[8,32,128]{2,1,0:T(8,128)S(1)}, u32[]{:S(2)}, u32[]{:S(2)}) collective-permute-start(f32[8,32,128]{2,1,0:T(8,128)S(1)} %copy-done.2), channel_id=1, source_target_pairs={{0,4},{4,0},{8,12},{12,8},{16,20},{20,16},{24,28},{28,24},{1,5},{5... | collective-permute-start | bytes 393224 | tf_op jit(solution)/shard_map/ppermute | solution.py:242
  12.0 1.7 %collective-permute-start = (s32[2,8]{1,0:T(2,128)S(1)}, s32[2,8]{1,0:T(2,128)S(1)}, u32[]{:S(2)}, u32[]{:S(2)}) collective-permute-start(s32[2,8]{1,0:T(2,128)S(1)} %bitcast.1), channel_id=1, source_target_pairs={{0,4},{4,0},{8,12},{12,8},{16,20},{20,16},{24,28},{28,24},{1,5},{5... | collective-permute-start | bytes 200 | tf_op jit(solution)/shard_map/ppermute | solution.py:242
  13.7 3.3 %collective-permute-start.7 = (f32[256,128]{1,0:T(8,128)S(1)}, f32[256,128]{1,0:T(8,128)S(1)}, u32[]{:S(2)}, u32[]{:S(2)}) collective-permute-start(f32[256,128]{1,0:T(8,128)S(1)} %get-tuple-element.17), channel_id=1, source_target_pairs={{1,13},{2,22},{3,31}} | collective-permute-start | bytes 393224 | tf_op jit(solution)/shard_map/ppermute | solution.py:239
  15.0 4.0 %collective-permute-start.6 = (f32[264,128]{1,0:T(8,128)S(1)}, f32[264,128]{1,0:T(8,128)S(1)}, u32[]{:S(2)}, u32[]{:S(2)}) collective-permute-start(f32[264,128]{1,0:T(8,128)S(1)} %shard_map.47.refs_5_), channel_id=1, source_target_pairs={{0,26},{4,30}} | collective-permute-start | bytes 405512 | tf_op jit(solution)/shard_map/ppermute | solution.py:239
  15.7 3.3 %collective-permute-start.5 = (f32[264,128]{1,0:T(8,128)S(1)}, f32[264,128]{1,0:T(8,128)S(1)}, u32[]{:S(2)}, u32[]{:S(2)}) collective-permute-start(f32[264,128]{1,0:T(8,128)S(1)} %shard_map.47.refs_5_), channel_id=1, source_target_pairs={{0,17},{4,21}} | collective-permute-start | bytes 405512 | tf_op jit(solution)/shard_map/ppermute | solution.py:239
  16.3 2.7 %collective-permute-start.4 = (f32[264,128]{1,0:T(8,128)S(1)}, f32[264,128]{1,0:T(8,128)S(1)}, u32[]{:S(2)}, u32[]{:S(2)}) collective-permute-start(f32[264,128]{1,0:T(8,128)S(1)} %shard_map.47.refs_5_), channel_id=1, source_target_pairs={{0,8},{4,12}} | collective-permute-start | bytes 405512 | tf_op jit(solution)/shard_map/ppermute | solution.py:239
  17.6 0.7 %collective-permute-start.8 = (f32[128,128]{1,0:T(8,128)S(1)}, f32[128,128]{1,0:T(8,128)S(1)}, u32[]{:S(2)}, u32[]{:S(2)}) collective-permute-start(f32[128,128]{1,0:T(8,128)S(1)} %get-tuple-element.18), channel_id=1, source_target_pairs={{13,8},{22,17},{31,26}} | collective-permute-start | bytes 196616 | tf_op jit(solution)/shard_map/ppermute | solution.py:239
  18.3 0.7 %collective-permute-start.9 = (f32[128,128]{1,0:T(8,128)S(1)}, f32[128,128]{1,0:T(8,128)S(1)}, u32[]{:S(2)}, u32[]{:S(2)}) collective-permute-start(f32[128,128]{1,0:T(8,128)S(1)} %get-tuple-element.19), channel_id=1, source_target_pairs={{13,12},{22,21},{31,30}} | collective-permute-start | bytes 196616 | tf_op jit(solution)/shard_map/ppermute | solution.py:239
  19.6 12.6 %collective-permute-start.12 = (f32[264,128]{1,0:T(8,128)S(1)}, f32[264,128]{1,0:T(8,128)S(1)}, u32[]{:S(2)}, u32[]{:S(2)}) collective-permute-start(f32[264,128]{1,0:T(8,128)S(1)} %shard_map.49.refs_4_), channel_id=1, source_target_pairs={{17,16},{21,20},{26,25},{30,29}} | collective-permute-start | bytes 405512 | tf_op jit(solution)/shard_map/ppermute | solution.py:239
  20.9 12.9 %collective-permute-start.11 = (f32[264,128]{1,0:T(8,128)S(1)}, f32[264,128]{1,0:T(8,128)S(1)}, u32[]{:S(2)}, u32[]{:S(2)}) collective-permute-start(f32[264,128]{1,0:T(8,128)S(1)} %shard_map.49.refs_4_), channel_id=1, source_target_pairs={{8,25},{12,29}} | collective-permute-start | bytes 405512 | tf_op jit(solution)/shard_map/ppermute | solution.py:239
  22.2 11.6 %collective-permute-start.10 = (f32[264,128]{1,0:T(8,128)S(1)}, f32[264,128]{1,0:T(8,128)S(1)}, u32[]{:S(2)}, u32[]{:S(2)}) collective-permute-start(f32[264,128]{1,0:T(8,128)S(1)} %shard_map.49.refs_4_), channel_id=1, source_target_pairs={{8,16},{12,20}} | collective-permute-start | bytes 405512 | tf_op jit(solution)/shard_map/ppermute | solution.py:239
  35.0 3.8 %collective-permute-start.16 = (f32[264,128]{1,0:T(8,128)S(1)}, f32[264,128]{1,0:T(8,128)S(1)}, u32[]{:S(2)}, u32[]{:S(2)}) collective-permute-start(f32[264,128]{1,0:T(8,128)S(1)} %shard_map.50.refs_3_), channel_id=1, source_target_pairs={{25,24},{29,28}} | collective-permute-start | bytes 405512 | tf_op jit(solution)/shard_map/ppermute | solution.py:239
  36.3 2.5 %collective-permute-start.15 = (f32[264,128]{1,0:T(8,128)S(1)}, f32[264,128]{1,0:T(8,128)S(1)}, u32[]{:S(2)}, u32[]{:S(2)}) collective-permute-start(f32[264,128]{1,0:T(8,128)S(1)} %shard_map.50.refs_3_), channel_id=1, source_target_pairs={{16,24},{20,28}} | collective-permute-start | bytes 405512 | tf_op jit(solution)/shard_map/ppermute | solution.py:239
  39.4 1.4 %collective-permute-start.17 = (f32[8,32,128]{2,1,0:T(8,128)S(1)}, f32[8,32,128]{2,1,0:T(8,128)S(1)}, u32[]{:S(2)}, u32[]{:S(2)}) collective-permute-start(f32[8,32,128]{2,1,0:T(8,128)S(1)} %get-tuple-element.22), channel_id=1, source_target_pairs={{0,4},{4,0},{8,12},{12,8},{16,20},{20,16},{24,28},{28,24},{1,5},{5... | collective-permute-start | bytes 393224 | tf_op jit(solution)/shard_map/ppermute | solution.py:242
  40.9 2.7 %collective-permute-start.20 = (f32[8,32,128]{2,1,0:T(8,128)S(1)}, f32[8,32,128]{2,1,0:T(8,128)S(1)}, u32[]{:S(2)}, u32[]{:S(2)}) collective-permute-start(f32[8,32,128]{2,1,0:T(8,128)S(1)} %add.3.refs_0_), channel_id=1, source_target_pairs={{0,3},{4,7},{8,11},{12,15},{16,19},{20,23},{24,27},{28,31}} | collective-permute-start | bytes 393224 | tf_op jit(solution)/shard_map/ppermute | solution.py:239
  41.5 2.0 %collective-permute-start.19 = (f32[8,32,128]{2,1,0:T(8,128)S(1)}, f32[8,32,128]{2,1,0:T(8,128)S(1)}, u32[]{:S(2)}, u32[]{:S(2)}) collective-permute-start(f32[8,32,128]{2,1,0:T(8,128)S(1)} %add.3.refs_0_), channel_id=1, source_target_pairs={{0,2},{4,6},{8,10},{12,14},{16,18},{20,22},{24,26},{28,30}} | collective-permute-start | bytes 393224 | tf_op jit(solution)/shard_map/ppermute | solution.py:239
  42.2 15.5 %collective-permute-start.18 = (f32[8,32,128]{2,1,0:T(8,128)S(1)}, f32[8,32,128]{2,1,0:T(8,128)S(1)}, u32[]{:S(2)}, u32[]{:S(2)}) collective-permute-start(f32[8,32,128]{2,1,0:T(8,128)S(1)} %add.3.refs_0_), channel_id=1, source_target_pairs={{0,1},{4,5},{8,9},{12,13},{16,17},{20,21},{24,25},{28,29}} | collective-permute-start | bytes 393224 | tf_op jit(solution)/shard_map/ppermute | solution.py:239
